TPU v7x, 512 devices: a whole 4x4x16 slice. The times are simulated.
512 devices in a mesh: pop: 16 (over z), tp: 32 (over y, x, core).
Axes of the slice: x: 4, y: 4, z: 16, core: 2. Of those that a mesh axis runs over, the one named last changes fastest.
Arguments:
- in_spikes: int32 [4, 15, 4096], replicated, may hold values 0 or 1
- w_in: bfloat16 [4096, 4096], P(None, 'tp'), may hold values from -0.1875 to 0.1875
- w_rec: bfloat16 [4096, 4096], P(None, 'tp'), may hold values from -0.1875 to 0.1875
- leak_rate: float32 [4096], P('tp'), may hold values from 0.5 to 0.95
- neuron_bias: float32 [4096], P('tp'), may hold values from -2.5 to 2.5
- readout: float32 [4096], P('tp'), may hold values from -0.1875 to 0.1875
- pert_table: bfloat16 [256, 4096], P(None, 'tp'), may hold values from -4 to 4
- pert_idx: int32 [512, 2], P('pop'), may hold values from 0 to 255
- member_ranks: int32 [512], P('pop'), may hold values from 0 to 511, each once
Outputs:
- returns: float32 [512], P('pop')
- grad_rec: bfloat16 [4096, 4096], P(None, 'tp')
Inputs may be any that keep to these rules, and one draw needn't show every extreme that they name: member_ranks holds each of 0 to 511 once.
All inputs are finite; a program needn't handle non-finite values.
Results may differ from a plain program's by a relative error of at most 0.0044.
Values may be sent and summed in bfloat16 or wider, within the bound.
A program may use at most 64 MiB of HBM per device.

v0:
```python
import jax
import jax.numpy as jnp
from jax import lax
from jax.sharding import PartitionSpec as P

sigma_scale = 0.01


def shards(
    in_spikes, w_in, w_rec, leak_rate, neuron_bias, readout, pert_table, pert_idx, member_ranks
):
    step_count, episodes, inputs = in_spikes.shape
    members_dev = pert_idx.shape[0]
    local_width = w_rec.shape[1]
    row_count = members_dev * episodes
    member_count = members_dev * lax.axis_size("pop")
    spike_input = in_spikes.astype(jnp.bfloat16).reshape(step_count * episodes, inputs)
    input_drive = jnp.dot(spike_input, w_in, preferred_element_type=jnp.float32) + neuron_bias
    input_drive = input_drive.reshape(step_count, episodes, local_width)
    post_side = jnp.take(pert_table, pert_idx[:, 1], axis=0).astype(jnp.float32)
    pre_local = jnp.take(pert_table, pert_idx[:, 0], axis=0)
    membrane = jnp.zeros((members_dev, episodes, local_width), jnp.float32)
    spikes = jnp.zeros((members_dev, episodes, local_width), jnp.bfloat16)
    readout_sum = jnp.zeros((members_dev, episodes), jnp.float32)
    for moment in range(step_count):
        current = input_drive[moment][None]
        if moment > 0:
            flat_spikes = spikes.reshape(row_count, local_width)
            recurrent = jnp.dot(
                lax.all_gather(flat_spikes, "tp", axis=1, tiled=True),
                w_rec,
                preferred_element_type=jnp.float32,
            )
            partial_proj = jnp.einsum(
                "men,mn->me", spikes, pre_local, preferred_element_type=jnp.float32
            )
            projection = lax.psum(partial_proj, "tp")
            current = (
                current
                + recurrent.reshape(members_dev, episodes, local_width)
                + sigma_scale * projection[:, :, None] * post_side[:, None, :]
            )
        membrane = leak_rate * (membrane - spikes.astype(jnp.float32)) + current
        spikes = jax.nn.sigmoid(4.0 * (membrane - 1.0)).astype(jnp.bfloat16)
        readout_sum = readout_sum + jnp.einsum(
            "men,n->me", spikes.astype(jnp.float32), readout, precision=lax.Precision.HIGHEST
        )
    returns = lax.psum(jnp.sum(readout_sum, axis=1), "tp") / (episodes * step_count)
    fitness = member_ranks.astype(jnp.float32) / (member_count - 1) - 0.5 + returns
    full_table = lax.all_gather(pert_table, "tp", axis=1, tiled=True)
    pre_side = jnp.take(full_table, pert_idx[:, 0], axis=0)
    weighted = pre_side.astype(jnp.float32) * fitness[:, None]
    partial_grad = jnp.dot(weighted.T, post_side, precision=lax.Precision.HIGHEST)
    grad_total = lax.psum(partial_grad, "pop")
    grad_rec = (grad_total * jnp.sqrt(12.0 / member_count)).astype(jnp.bfloat16)
    return (returns, grad_rec)


def solution(mesh):
    placed = (
        P(),
        P(None, "tp"),
        P(None, "tp"),
        P("tp"),
        P("tp"),
        P("tp"),
        P(None, "tp"),
        P("pop", None),
        P("pop"),
    )
    return jax.shard_map(
        shards, mesh=mesh, in_specs=placed, out_specs=(P("pop"), P(None, "tp")), check_vma=False
    )
```

profile of v0, /device:TPU:2, one launch (start us, length us, event | category | flops | bytes accessed | tf_op | source)
XLA Modules:
  0.0 627.7 jit_solution(11795909745084561978)
XLA Ops:
  7.3 1.5 convert_element_type.59
  8.7 0.3 copy.12
  9.2 1.5 convolution_add_fusion
  10.8 0.7 divide_convert_fusion.5
  11.7 0.6 gather_fusion.2
  12.4 0.6 gather_fusion.1
  13.3 124.6 %psum.35 = f32[32,15]{1,0:T(8,128)S(1)} all-reduce(f32[32,15]{1,0:T(8,128)S(1)} %bitcast.55), channel_id=1, replica_groups=mesh['pop'=16,'tp'=32] {'tp'}, use_global_device_ids=true, to_apply=%region_0.0 | all-reduce | flops 480 | bytes 3840 | tf_op jit(solution)/shard_map/psum | solution.py:37
  138.1 4.0 divide_convert_fusion.4
  142.2 0.7 all-gather.11.cloned.1.call-update
  143.3 124.4 %psum.36 = f32[32,15]{1,0:T(8,128)S(1)} all-reduce(f32[32,15]{1,0:T(8,128)S(1)} %bitcast.56), channel_id=1, replica_groups=mesh['pop'=16,'tp'=32] {'tp'}, use_global_device_ids=true, to_apply=%region_1.3 | all-reduce | flops 480 | bytes 3840 | tf_op jit(solution)/shard_map/psum | solution.py:37
  267.9 4.0 divide_convert_fusion.3
  272.0 2.8 gather_fusion
  274.8 0.2 fusion.19
  275.3 0.3 divide_convert_fusion.1
  275.6 0.2 fusion.17
  276.0 0.2 fusion.21
  276.6 124.1 %psum.37 = f32[32,15]{1,0:T(8,128)S(1)} all-reduce(f32[32,15]{1,0:T(8,128)S(1)} %bitcast.54), channel_id=1, replica_groups=mesh['pop'=16,'tp'=32] {'tp'}, use_global_device_ids=true, to_apply=%region_2.4 | all-reduce | flops 480 | bytes 3840 | tf_op jit(solution)/shard_map/psum | solution.py:37
  400.7 3.3 fusion.42
  404.2 0.2 fusion.15
  404.6 62.7 %psum.38 = f32[32]{0:T(128)S(1)} all-reduce(f32[32]{0:T(128)S(1)} %fusion.30), channel_id=1, replica_groups=mesh['pop'=16,'tp'=32] {'tp'}, use_global_device_ids=true, to_apply=%region_4.6 | all-reduce | flops 32 | bytes 256 | tf_op jit(solution)/shard_map/psum | solution.py:48
  467.3 0.5 add_add_fusion.3
  467.8 3.2 fusion
  471.0 147.4 %all-reduce.2.cloned.1.call-done = f32[4096,128]{1,0:T(8,128)} async-done(((f32[4096,128]{1,0:T(8,128)}), f32[4096,128]{1,0:T(8,128)}) %all-reduce.2.cloned.1.call-update) | async-done | bytes 2097168 | tf_op jit(solution)/shard_map/psum | solution.py:54
  618.5 2.7 multiply_convert_fusion
  (62 shorter events, 2.7 us)
Async XLA Ops:
  7.2 130.9 %copy-start = (bf16[4096,128]{1,0:T(8,128)(2,1)S(1)}, bf16[4096,128]{1,0:T(8,128)(2,1)}, u32[]{:S(2)}) copy-start(bf16[4096,128]{1,0:T(8,128)(2,1)} %param.13) | copy-start | bytes 3145732
  7.2 3.6 copy-start.3
  7.2 4.4 copy-start.4
  7.2 4.5 copy-start.1
  7.2 130.9 %all-gather.5.cloned.1.call-start = ((), (), s32[]{:S(2)}) async-start(), calls=%async_computation | async-start | bytes 4055040 | tf_op jit(solution)/shard_map/all_gather | solution.py:30
  11.6 256.3 %all-gather.7.cloned.1.call-start = ((), (), s32[]{:S(2)}) async-start(), calls=%async_computation.1 | async-start | bytes 4055040 | tf_op jit(solution)/shard_map/all_gather | solution.py:30
  142.1 129.9 %all-gather.11.cloned.1.call-start = ((), (), s32[]{:S(2)}) async-start(), calls=%async_computation.3 | async-start | bytes 2162688 | tf_op jit(solution)/shard_map/all_gather | solution.py:50
  142.8 257.8 %all-gather.9.cloned.1.call-start = ((), (), s32[]{:S(2)}) async-start(), calls=%async_computation.2 | async-start | bytes 4055040 | tf_op jit(solution)/shard_map/all_gather | solution.py:30
  267.9 7.0 %copy-start.2 = (f32[128]{0:T(128)S(1)}, f32[128]{0:T(128)}, u32[]{:S(2)}) copy-start(f32[128]{0:T(128)} %param.16) | copy-start | bytes 1540
  271.9 346.6 %all-reduce.2.cloned.1.call-start = ((), (), s32[]{:S(2)}) async-start(), calls=%async_computation.4 | async-start | bytes 4194304 | tf_op jit(solution)/shard_map/psum | solution.py:54
  276.4 190.9 %copy-start.5 = (s32[32]{0:T(128)S(1)}, s32[32]{0:T(128)}, u32[]{:S(2)}) copy-start(s32[32]{0:T(128)} %param.19) | copy-start | bytes 388
Sparse Core Ops, SparseCore 0:
  11.7 68.1 all-gather.4
  142.2 67.1 all-gather.6
  212.4 59.5 all-gather.10
  275.5 63.4 all-gather.8
  471.1 147.2 all-reduce.1
where the time goes:
time: 628 us
  blocking collectives  436 us (69%)
  waiting for transfers between devices  148 us (24%)
  matrix products  17.5 us (3%)
  between operations  14.1 us (2%)
  other arithmetic  6.33 us (1%)
    psum x3, blocking collectives, shards(): projection = lax.psum(partial_proj, 'tp')  373 us
    psum x1, waiting for transfers between devices, shards(): grad_total = lax.psum(partial_grad, 'pop')  147 us
    psum x1, blocking collectives, shards(): lax.psum(jnp.sum(readout_sum, axis=1), 'tp') / (episodes * step_count)  62.7 us
  transfers between devices with their start and end apart: 5, of which 1 were waited for; matrix products, arithmetic and copies ran while one was open for 2% of the time, Pallas kernels for 0%

commit v1 on v0

--- a/solution.py
+++ b/solution.py
@@ -51,7 +51,14 @@
     pre_side = jnp.take(full_table, pert_idx[:, 0], axis=0)
     weighted = pre_side.astype(jnp.float32) * fitness[:, None]
     partial_grad = jnp.dot(weighted.T, post_side, precision=lax.Precision.HIGHEST)
-    grad_total = lax.psum(partial_grad, "pop")
+    count_all = lax.axis_size("pop")
+    grad_total, later = (partial_grad, 0)
+    while 1 << later < count_all:
+        outer = lax.ppermute(
+            grad_total, "pop", perm=[(q, q ^ 1 << later) for q in range(count_all)]
+        )
+        grad_total = grad_total + outer
+        later = later + 1
     grad_rec = (grad_total * jnp.sqrt(12.0 / member_count)).astype(jnp.bfloat16)
     return (returns, grad_rec)
 

time: 628 us -> 1050 us (1.67)
  the two profiles are of different devices: /device:TPU:2 before, /device:TPU:1 now
where the time goes in v1:
time: 1050 us
  waiting for transfers between devices  453 us (43%)
  blocking collectives  441 us (42%)
  starting transfers between devices  118 us (11%)
  matrix products  15 us (1%)
  between operations  14.2 us (1%)
    ppermute x4, waiting for transfers between devices, shards(): lax.ppermute(grad_total, 'pop', perm=[(q, q ^ 1 << later) for q in range(...  452 us
    psum x3, blocking collectives, shards(): projection = lax.psum(partial_proj, 'tp')  373 us
    ppermute x4, starting transfers between devices, shards(): lax.ppermute(grad_total, 'pop', perm=[(q, q ^ 1 << later) for q in range(...  118 us
    psum x1, blocking collectives, shards(): lax.psum(jnp.sum(readout_sum, axis=1), 'tp') / (episodes * step_count)  67.7 us
  transfers between devices with their start and end apart: 8, of which 5 were waited for; matrix products, arithmetic and copies ran while one was open for 1% of the time, Pallas kernels for 0%

profile of v1, /device:TPU:1, one launch (start us, length us, event | category | flops | bytes accessed | tf_op | source)
XLA Modules:
  0.0 1053.0 jit_solution(747721626378910293)
XLA Ops:
  7.2 1.5 convert_element_type.59
  9.7 0.7 divide_convert_fusion.5
  10.6 0.6 gather_fusion.2
  11.3 0.6 gather_fusion.1
  12.1 125.4 %psum.28 = f32[32,15]{1,0:T(8,128)S(1)} all-reduce(f32[32,15]{1,0:T(8,128)S(1)} %bitcast.55), channel_id=1, replica_groups=mesh['pop'=16,'tp'=32] {'tp'}, use_global_device_ids=true, to_apply=%region_0.0 | all-reduce | flops 480 | bytes 3840 | tf_op jit(solution)/shard_map/psum | solution.py:37
  137.8 4.0 divide_convert_fusion.4
  141.8 0.7 all-gather.11.cloned.1.call-update
  143.0 124.5 %psum.29 = f32[32,15]{1,0:T(8,128)S(1)} all-reduce(f32[32,15]{1,0:T(8,128)S(1)} %bitcast.56), channel_id=1, replica_groups=mesh['pop'=16,'tp'=32] {'tp'}, use_global_device_ids=true, to_apply=%region_1.3 | all-reduce | flops 480 | bytes 3840 | tf_op jit(solution)/shard_map/psum | solution.py:37
  267.6 4.0 divide_convert_fusion.3
  271.7 0.8 all-gather.11.cloned.1.call-done
  272.4 2.8 gather_fusion
  277.0 123.4 %psum.30 = f32[32,15]{1,0:T(8,128)S(1)} all-reduce(f32[32,15]{1,0:T(8,128)S(1)} %bitcast.54), channel_id=1, replica_groups=mesh['pop'=16,'tp'=32] {'tp'}, use_global_device_ids=true, to_apply=%region_2.4 | all-reduce | flops 480 | bytes 3840 | tf_op jit(solution)/shard_map/psum | solution.py:37
  400.4 3.3 fusion.42
  404.4 67.7 %psum.31 = f32[32]{0:T(128)S(1)} all-reduce(f32[32]{0:T(128)S(1)} %fusion.30), channel_id=1, replica_groups=mesh['pop'=16,'tp'=32] {'tp'}, use_global_device_ids=true, to_apply=%region_4.6 | all-reduce | flops 32 | bytes 256 | tf_op jit(solution)/shard_map/psum | solution.py:48
  472.6 1.9 fusion
  474.5 2.6 collective-permute-start
  477.1 45.8 %collective-permute-done = f32[4096,128]{1,0:T(8,128)S(1)} collective-permute-done((f32[4096,128]{1,0:T(8,128)S(1)}, f32[4096,128]{1,0:T(8,128)S(1)}, u32[]{:S(2)}, u32[]{:S(2)}) %collective-permute-start) | collective-permute-done | bytes 2097184 | tf_op jit(solution)/shard_map/ppermute | solution.py:57
  523.1 4.1 collective-permute-start.1
  527.2 90.3 %collective-permute-done.1 = f32[4096,128]{1,0:T(8,128)S(1)} collective-permute-done((f32[4096,128]{1,0:T(8,128)S(1)}, f32[4096,128]{1,0:T(8,128)S(1)}, u32[]{:S(2)}, u32[]{:S(2)}) %collective-permute-start.1) | collective-permute-done | bytes 2097184 | tf_op jit(solution)/shard_map/ppermute | solution.py:57
  617.7 8.1 collective-permute-start.2
  625.9 225.2 %collective-permute-done.2 = f32[4096,128]{1,0:T(8,128)S(1)} collective-permute-done((f32[4096,128]{1,0:T(8,128)S(1)}, f32[4096,128]{1,0:T(8,128)S(1)}, u32[]{:S(2)}, u32[]{:S(2)}) %collective-permute-start.2) | collective-permute-done | bytes 2097184 | tf_op jit(solution)/shard_map/ppermute | solution.py:57
  851.3 103.4 %collective-permute-start.3 = (f32[4096,128]{1,0:T(8,128)S(1)}, f32[4096,128]{1,0:T(8,128)S(1)}, u32[]{:S(2)}, u32[]{:S(2)}) collective-permute-start(f32[4096,128]{1,0:T(8,128)S(1)} %add.214), channel_id=1, source_target_pairs={{0,256},{32,288},{64,320},{96,352},{128,384},{160,416},{192,448},{... | collective-permute-start | bytes 6291464 | tf_op jit(solution)/shard_map/ppermute | solution.py:57
  954.6 90.6 %collective-permute-done.3 = f32[4096,128]{1,0:T(8,128)S(1)} collective-permute-done((f32[4096,128]{1,0:T(8,128)S(1)}, f32[4096,128]{1,0:T(8,128)S(1)}, u32[]{:S(2)}, u32[]{:S(2)}) %collective-permute-start.3) | collective-permute-done | bytes 2097184 | tf_op jit(solution)/shard_map/ppermute | solution.py:57
  1045.2 1.2 multiply_convert_fusion
  (74 shorter events, 5.6 us)
Async XLA Ops:
  7.2 130.6 %copy-start = (bf16[4096,128]{1,0:T(8,128)(2,1)S(1)}, bf16[4096,128]{1,0:T(8,128)(2,1)}, u32[]{:S(2)}) copy-start(bf16[4096,128]{1,0:T(8,128)(2,1)} %param.13) | copy-start | bytes 3145732
  7.2 2.1 copy-start.1
  7.2 2.1 copy-start.6
  7.2 130.6 %all-gather.5.cloned.1.call-start = ((), (), s32[]{:S(2)}) async-start(), calls=%async_computation | async-start | bytes 4055040 | tf_op jit(solution)/shard_map/all_gather | solution.py:30
  8.8 0.8 copy-start.4
  9.1 1.4 copy-start.5
  9.1 1.5 copy-start.2
  10.4 257.2 %all-gather.7.cloned.1.call-start = ((), (), s32[]{:S(2)}) async-start(), calls=%async_computation.1 | async-start | bytes 4055040 | tf_op jit(solution)/shard_map/all_gather | solution.py:30
  141.8 130.7 %all-gather.11.cloned.1.call-start = ((), (), s32[]{:S(2)}) async-start(), calls=%async_computation.3 | async-start | bytes 2162688 | tf_op jit(solution)/shard_map/all_gather | solution.py:50
  142.5 257.9 %all-gather.9.cloned.1.call-start = ((), (), s32[]{:S(2)}) async-start(), calls=%async_computation.2 | async-start | bytes 4055040 | tf_op jit(solution)/shard_map/all_gather | solution.py:30
  271.6 3.6 copy-start.3
  400.4 71.6 %copy-start.7 = (s32[32]{0:T(128)S(1)}, s32[32]{0:T(128)}, u32[]{:S(2)}) copy-start(s32[32]{0:T(128)} %param.19) | copy-start | bytes 388
  474.5 48.4 %collective-permute-start = (f32[4096,128]{1,0:T(8,128)S(1)}, f32[4096,128]{1,0:T(8,128)S(1)}, u32[]{:S(2)}, u32[]{:S(2)}) collective-permute-start(f32[4096,128]{1,0:T(8,128)S(1)} %fusion), channel_id=1, source_target_pairs={{0,32},{32,0},{64,96},{96,64},{128,160},{160,128},{192,224},{224,1... | collective-permute-start | bytes 6291464 | tf_op jit(solution)/shard_map/ppermute | solution.py:57
  523.1 94.4 %collective-permute-start.1 = (f32[4096,128]{1,0:T(8,128)S(1)}, f32[4096,128]{1,0:T(8,128)S(1)}, u32[]{:S(2)}, u32[]{:S(2)}) collective-permute-start(f32[4096,128]{1,0:T(8,128)S(1)} %add.212), channel_id=1, source_target_pairs={{0,64},{32,96},{64,0},{96,32},{128,192},{160,224},{192,128},{224,1... | collective-permute-start | bytes 6291464 | tf_op jit(solution)/shard_map/ppermute | solution.py:57
  617.7 233.3 %collective-permute-start.2 = (f32[4096,128]{1,0:T(8,128)S(1)}, f32[4096,128]{1,0:T(8,128)S(1)}, u32[]{:S(2)}, u32[]{:S(2)}) collective-permute-start(f32[4096,128]{1,0:T(8,128)S(1)} %add.213), channel_id=1, source_target_pairs={{0,128},{32,160},{64,192},{96,224},{128,0},{160,32},{192,64},{224,... | collective-permute-start | bytes 6291464 | tf_op jit(solution)/shard_map/ppermute | solution.py:57
  851.3 193.9 %collective-permute-start.3 = (f32[4096,128]{1,0:T(8,128)S(1)}, f32[4096,128]{1,0:T(8,128)S(1)}, u32[]{:S(2)}, u32[]{:S(2)}) collective-permute-start(f32[4096,128]{1,0:T(8,128)S(1)} %add.214), channel_id=1, source_target_pairs={{0,256},{32,288},{64,320},{96,352},{128,384},{160,416},{192,448},{... | collective-permute-start | bytes 6291464 | tf_op jit(solution)/shard_map/ppermute | solution.py:57
Sparse Core Ops, SparseCore 0:
  11.7 69.6 all-gather.4
  141.9 67.7 all-gather.6
  212.8 59.6 all-gather.10
  275.9 63.5 all-gather.8
